TPU v7x, 256 devices: a whole 4x4x8 slice. The times are simulated.
256 devices in a mesh: row: 16 (over x_lo, z), col: 16 (over x_hi, y, core).
Axes of the slice: x: 4 (x_hi: 2, x_lo: 2; x = x_hi * 2 + x_lo), y: 4, z: 8, core: 2. Of those that a mesh axis runs over, the one named last changes fastest.
Arguments:
- hidden_in: bfloat16 [12288, 5120], P('row', 'col'), may hold values from -6 to 6
- modulation: bfloat16 [48, 3, 5120], P(None, None, 'col'), may hold values from -3 to 3
- w_qkv: bfloat16 [5120, 12288], P('row', 'col'), may hold values from -0.078125 to 0.078125
- w_out: bfloat16 [4096, 5120], P('row', 'col'), may hold values from -0.09375 to 0.09375
- prefix_cache: bfloat16 [16, 256, 8192], P('row', None, 'col'), may hold values from -48 to 48
- req_group: int32 [48], replicated, may hold values from 0 to 3
- req_len: int32 [48], replicated, may hold values from 1 to 672, 12288 in all
- owner: int32 [4], replicated, may hold values from 0 to 15, as said below
Outputs:
- hidden_out: bfloat16 [12288, 5120], P('row', 'col')
- suffix_keys: bfloat16 [12288, 4096], P('row', 'col')
- suffix_values: bfloat16 [12288, 4096], P('row', 'col')
Inputs may be any that keep to these rules, and one draw needn't show every extreme that they name: `owner`: the 4 slots are distinct; slot 0 and slot 16 - 1 always hold a group.
All inputs are finite; a program needn't handle non-finite values.
Results may differ from a plain program's by a relative error of at most 0.006.
Values may be sent and summed in bfloat16 or wider, within the bound.
A program may use at most 192 MiB of HBM per device.

v0:
```python
import math
import jax
import jax.numpy as jnp
from jax import lax
from jax.sharding import PartitionSpec as P

HD = 128
neg_fill = -1e30


def with_halo(block, sides, width):
    for axis, dim in sides:
        count = lax.axis_size(axis)
        forward = [(i, i + 1) for i in range(count - 1)]
        backward = [(target, source) for source, target in forward]
        low = lax.ppermute(
            lax.slice_in_dim(block, block.shape[dim] - width, None, axis=dim), axis, forward
        )
        high = lax.ppermute(lax.slice_in_dim(block, 0, width, axis=dim), axis, backward)
        block = jnp.concatenate([low, block, high], axis=dim)
    return block


def request_of(positions, req_len):
    starts = jnp.cumsum(req_len) - req_len
    inside = (starts[None, :] <= positions[:, None]).astype(jnp.int32)
    return jnp.sum(inside, axis=1) - 1


def attend(running, queries, key_block, value_block, allowed):
    largest, denominator, summed = running
    scores = jnp.einsum("thd,khd->thk", queries, key_block, preferred_element_type=jnp.float32)
    scores = scores * (1.0 / math.sqrt(queries.shape[-1]))
    widened = allowed[:, None, :]
    scores = jnp.where(widened, scores, neg_fill)
    new_largest = jnp.maximum(largest, jnp.max(scores, axis=2))
    weights = jnp.where(widened, jnp.exp(scores - new_largest[:, :, None]), 0.0)
    rescale = jnp.exp(largest - new_largest)
    denominator = denominator * rescale + jnp.sum(weights, axis=2)
    summed = summed * rescale[:, :, None] + jnp.einsum(
        "thk,khd->thd",
        weights.astype(jnp.bfloat16),
        value_block,
        preferred_element_type=jnp.float32,
    )
    return (new_largest, denominator, summed)


def shards(hidden_in, modulation, w_qkv, w_out, prefix_cache, req_group, req_len, owner):
    token_rows = hidden_in.shape[0]
    full_hidden, full_modulation = (
        lax.all_gather(hidden_in, "col", axis=1, tiled=True),
        lax.all_gather(modulation, "col", axis=2, tiled=True),
    )
    full_width = full_hidden.shape[1]
    requests = req_len.shape[0]
    row_index = lax.axis_index("row")
    positions = row_index * token_rows + jnp.arange(token_rows, dtype=jnp.int32)
    request_id = request_of(positions, req_len)
    matches = request_id[:, None] == jnp.arange(requests, dtype=jnp.int32)[None, :]
    onehot = matches.astype(jnp.bfloat16)
    per_token = jnp.dot(
        onehot,
        full_modulation.reshape(requests, 3 * full_width),
        preferred_element_type=jnp.float32,
    )
    shift_rows = per_token[:, :full_width]
    scale_rows = per_token[:, full_width : 2 * full_width]
    gate_rows = jnp.dot(onehot, modulation[:, 2, :], preferred_element_type=jnp.float32)
    token_group = jnp.sum(jnp.where(matches, req_group[None, :], 0), axis=1)
    hidden_f = full_hidden.astype(jnp.float32)
    average = jnp.mean(hidden_f, axis=1, keepdims=True)
    centred = hidden_f - average
    variance = jnp.mean(centred * centred, axis=1, keepdims=True)
    modulated = (centred * lax.rsqrt(variance + 1e-06) * (1.0 + scale_rows) + shift_rows).astype(
        jnp.bfloat16
    )
    projected_qkv = jnp.dot(
        modulated,
        lax.all_gather(w_qkv, "row", axis=0, tiled=True),
        preferred_element_type=jnp.float32,
    )
    local_heads = w_qkv.shape[1] // (3 * HD)
    projected_qkv = projected_qkv.astype(jnp.bfloat16).reshape(token_rows, local_heads, 3, HD)
    queries = projected_qkv[:, :, 0]
    new_keys = projected_qkv[:, :, 1]
    new_values = projected_qkv[:, :, 2]
    key_value = projected_qkv[:, :, 1:].reshape(token_rows, local_heads * 2 * HD)
    surrounded = with_halo(key_value, (("row", 0),), token_rows)
    running = (
        jnp.full((token_rows, local_heads), neg_fill, jnp.float32),
        jnp.zeros((token_rows, local_heads), jnp.float32),
        jnp.zeros((token_rows, local_heads, HD), jnp.float32),
    )

    def slot_attend(carried, slot_data, group_number):
        present = token_group == group_number
        arranged = slot_data.reshape(slot_data.shape[0], local_heads, 2, HD)
        allowed = jnp.broadcast_to(present[:, None], (token_rows, slot_data.shape[0]))
        return attend(carried, queries, arranged[:, :, 0], arranged[:, :, 1], allowed)

    group_numbers = jnp.arange(owner.shape[0], dtype=jnp.int32)
    slot_block = lax.all_gather(prefix_cache, "row", axis=0, tiled=True)

    def one_slot(offset, current):
        group_number = jnp.sum(jnp.where(owner == offset, group_numbers + 1, 0)) - 1
        slot_data = lax.dynamic_index_in_dim(slot_block, offset, 0, keepdims=False)
        return slot_attend(current, slot_data, group_number)

    running = lax.fori_loop(0, slot_block.shape[0], one_slot, running)
    near_pairs = surrounded.reshape(3 * token_rows, local_heads, 2, HD)
    key_pos = (row_index - 1) * token_rows + jnp.arange(3 * token_rows, dtype=jnp.int32)
    key_req = request_of(key_pos, req_len)
    inside_range = key_pos < jnp.sum(req_len)
    near_mask = (key_req[None, :] == request_id[:, None]) & inside_range[None, :]
    running = attend(running, queries, near_pairs[:, :, 0], near_pairs[:, :, 1], near_mask)
    largest, denominator, summed = running
    attended = (
        (summed / denominator[:, :, None])
        .astype(jnp.bfloat16)
        .reshape(token_rows, local_heads * HD)
    )
    out_weight = lax.all_gather(w_out, "row", axis=0, tiled=True)
    projected = jnp.dot(
        lax.all_gather(attended, "col", axis=1, tiled=True),
        out_weight,
        preferred_element_type=jnp.float32,
    )
    hidden_out = (hidden_in.astype(jnp.float32) + gate_rows * projected).astype(jnp.bfloat16)
    return (
        hidden_out,
        new_keys.reshape(token_rows, local_heads * HD),
        new_values.reshape(token_rows, local_heads * HD),
    )


def solution(mesh):
    return jax.shard_map(
        shards,
        mesh=mesh,
        in_specs=(
            P("row", "col"),
            P(None, None, "col"),
            P("row", "col"),
            P("row", "col"),
            P("row", None, "col"),
            P(),
            P(),
            P(),
        ),
        out_specs=(P("row", "col"), P("row", "col"), P("row", "col")),
        check_vma=False,
    )
```

profile of v0, /device:TPU:1, one launch (start us, length us, event | category | flops | bytes accessed | tf_op | source)
XLA Modules:
  0.0 497.8 jit_solution(4544151833377507003)
XLA Ops:
  7.2 1.8 copy.59
  12.7 1.3 fusion.60
  15.0 0.7 select_reduce_fusion
  15.7 2.9 compare_and_fusion
  18.6 61.9 %all-gather.11.cloned.1.call-done = bf16[48,3,5120]{0,1,2:T(4,128)(2,1)} async-done(((bf16[48,3,320]{0,1,2:T(4,128)(2,1)}), bf16[48,3,5120]{0,1,2:T(4,128)(2,1)}) %all-gather.11.cloned.1.call-update) | async-done | bytes 1474576 | tf_op jit(solution)/shard_map/all_gather | solution.py:53
  80.4 7.7 %copy.60 = bf16[48,3,5120]{2,1,0:T(4,128)(2,1)S(1)} copy(bf16[48,3,5120]{0,1,2:T(4,128)(2,1)} %all-gather.11.cloned.1.call-done) | data formatting | bytes 2949120 | tf_op jit(solution)/shard_map/all_gather | solution.py:53
  88.8 18.8 %fusion.48 = f32[768,15360]{1,0:T(8,128)} fusion(bf16[48,15360]{1,0:T(8,128)(2,1)S(1)} %bitcast.111, s32[768]{0:T(1024)S(1)} %broadcast_add_fusion.1), kind=kOutput, calls=%fused_computation.61 | convolution fusion | flops 1132498944 | bytes 48663552 | tf_op jit(solution)/shard_map/dot_general | solution.py:62
  107.5 49.4 %all-gather.9.cloned.1.call-done = bf16[768,5120]{0,1:T(8,128)(2,1)} async-done(((bf16[768,320]{0,1:T(8,128)(2,1)}), bf16[768,5120]{0,1:T(8,128)(2,1)}) %all-gather.9.cloned.1.call-update) | async-done | bytes 7864336 | tf_op jit(solution)/shard_map/all_gather | solution.py:52
  156.9 10.7 %copy.58 = bf16[768,5120]{1,0:T(8,128)(2,1)} copy(bf16[768,5120]{0,1:T(8,128)(2,1)} %all-gather.9.cloned.1.call-done) | data formatting | bytes 15728640 | tf_op jit(solution)/shard_map/all_gather | solution.py:52
  167.6 4.5 convert_reduce_fusion
  172.1 1.0 copy-done
  173.1 2.2 fusion.17
  175.3 76.6 %all-gather.13.cloned.1.call-done = bf16[5120,768]{1,0:T(8,128)(2,1)} async-done(((bf16[320,768]{1,0:T(8,128)(2,1)}), bf16[5120,768]{1,0:T(8,128)(2,1)}) %all-gather.13.cloned.1.call-update) | async-done | bytes 7864336 | tf_op jit(solution)/shard_map/all_gather | solution.py:80
  251.9 21.3 %fusion.29 = bf16[768,768]{0,1:T(8,128)(2,1)S(1)} fusion(bf16[5120,768]{1,0:T(8,128)(2,1)} %all-gather.13.cloned.1.call-done, bf16[768,5120]{1,0:T(8,128)(2,1)} %copy.58, f32[768,15360]{1,0:T(8,128)} %fusion.48, f32[768]{0:T(1024)S(1)} %add_rsqrt_fusion, f32[768]{0:T(1024)S(1)} %broadcast_multiply_fusion), kind=kOutput, calls=%fused_computation.46 | convolution fusion | flops 6067912704 | bytes 48371712 | tf_op jit(solution)/shard_map/dot_general | solution.py:78
  273.2 1.0 slice.63
  274.3 2.2 collective-permute-start
  276.4 1.5 collective-permute-start.1
  277.9 1.0 fusion.59
  279.1 51.5 %all-gather.7.cloned.1.call-done = bf16[16,256,512]{2,1,0:T(8,128)(2,1)} async-done(((bf16[1,256,512]{2,1,0:T(8,128)(2,1)}), bf16[16,256,512]{2,1,0:T(8,128)(2,1)}) %all-gather.7.cloned.1.call-update) | async-done | bytes 4194320 | tf_op jit(solution)/shard_map/all_gather | solution.py:103
  330.6 58.0 %while.20 = (s32[]{:T(128)}, f32[768,2]{0,1:T(2,128)S(1)}, f32[768,2]{0,1:T(2,128)S(1)}, f32[768,2,128]{0,2,1:T(8,128)S(1)}, s32[4]{0:T(128)S(1)}, /*index=5*/s3...) while((s32[]{:T(128)}, f32[768,2]{0,1:T(2,128)S(1)}, ...), condition=%wide.region_9.10_spmd.clone, body=%wide.region_5.9_spmd.clone.sunk | while | flops 205463824 | bytes 8100517 | solution.py:110
  331.8 1.0 constant_dynamic-slice_fusion.2
  335.5 1.0 constant_dynamic-slice_fusion.2
  339.1 1.0 constant_dynamic-slice_fusion.2
  342.7 1.0 constant_dynamic-slice_fusion.2
  346.3 1.0 constant_dynamic-slice_fusion.2
  350.0 1.0 constant_dynamic-slice_fusion.2
  353.6 1.0 constant_dynamic-slice_fusion.2
  357.2 1.0 constant_dynamic-slice_fusion.2
  360.8 1.0 constant_dynamic-slice_fusion.2
  364.4 1.0 constant_dynamic-slice_fusion.2
  368.1 1.0 constant_dynamic-slice_fusion.2
  371.7 1.0 constant_dynamic-slice_fusion.2
  375.3 1.0 constant_dynamic-slice_fusion.2
  379.0 1.0 constant_dynamic-slice_fusion.2
  382.6 1.0 constant_dynamic-slice_fusion.2
  386.2 1.0 constant_dynamic-slice_fusion.2
  388.6 1.6 copy.80
  390.3 2.3 copy.65
  392.6 2.3 copy.66
  394.9 1.5 pad_maximum_fusion
  396.4 4.2 fusion.21
  400.7 4.0 fusion.22
  404.7 5.7 %fusion.44 = bf16[768,2,128]{0,2,1:T(8,128)(2,1)} fusion(f32[2,2304,768]{2,1,0:T(8,128)S(1)} %get-tuple-element.301, f32[768,2]{0,1:T(2,128)S(1)} %max.13, pred[768,2304]{0,1:T(8,128)(4,1)S(1)} %copy-done.1, bf16[2304,2,2,128]{3,0,1,2:T(8,128)(2,1)} %copy-done.3, f32[768,2,128]{0,2,1:T(8,128)S(1)} %get-tuple-element.225, ...), kind=kOutput, calls=%fused_computation.56 | convolution fusion | flops 924450816 | bytes 18302976 | tf_op jit(solution)/shard_map/thk,khd->thd/dot_general | solution.py:40
  410.5 1.1 fusion.49
  411.6 0.9 copy.74
  412.5 0.9 copy.75
  413.4 71.0 %all-gather.15.cloned.1.call-done = bf16[768,4096]{0,1:T(8,128)(2,1)} async-done(((bf16[768,256]{0,1:T(8,128)(2,1)}), bf16[768,4096]{0,1:T(8,128)(2,1)}) %all-gather.15.cloned.1.call-update) | async-done | bytes 6291472 | tf_op jit(solution)/shard_map/all_gather | solution.py:125
  484.4 6.6 %fusion.36 = bf16[768,320]{0,1:T(8,128)(2,1)} fusion(f32[768,320]{0,1:T(8,128)S(1)} %fusion.49, bf16[4096,320]{0,1:T(8,128)(2,1)} %all-gather.17.cloned.1.call-done, bf16[768,4096]{0,1:T(8,128)(2,1)} %all-gather.15.cloned.1.call-done, bf16[768,320]{0,1:T(8,128)(2,1)} %param.10), kind=kOutput, calls=%fused_computation.50 | convolution fusion | flops 2014248960 | bytes 10878976 | tf_op jit(solution)/shard_map/dot_general | solution.py:124
  (191 shorter events, 37.5 us)
Async XLA Ops:
  7.2 73.3 %all-gather.11.cloned.1.call-start = ((), (), s32[]{:S(2)}) async-start(), calls=%async_computation.2 | async-start | bytes 5570560 | tf_op jit(solution)/shard_map/all_gather | solution.py:53
  9.1 147.9 %all-gather.9.cloned.1.call-start = ((), (), s32[]{:S(2)}) async-start(), calls=%async_computation.1 | async-start | bytes 8355840 | tf_op jit(solution)/shard_map/all_gather | solution.py:52
  9.8 242.1 %all-gather.13.cloned.1.call-start = ((), (), s32[]{:S(2)}) async-start(), calls=%async_computation.3 | async-start | bytes 8355840 | tf_op jit(solution)/shard_map/all_gather | solution.py:80
  10.5 320.1 %all-gather.7.cloned.1.call-start = ((), (), s32[]{:S(2)}) async-start(), calls=%async_computation | async-start | bytes 4456448 | tf_op jit(solution)/shard_map/all_gather | solution.py:103
  11.1 402.3 %all-gather.17.cloned.1.call-start = ((), (), s32[]{:S(2)}) async-start(), calls=%async_computation.5 | async-start | bytes 2785280 | tf_op jit(solution)/shard_map/all_gather | solution.py:123
  11.7 472.7 %all-gather.15.cloned.1.call-start = ((), (), s32[]{:S(2)}) async-start(), calls=%async_computation.4 | async-start | bytes 6684672 | tf_op jit(solution)/shard_map/all_gather | solution.py:125
  167.6 5.5 %copy-start = (bf16[768,5120]{1,0:T(8,128)(2,1)S(1)}, bf16[768,5120]{1,0:T(8,128)(2,1)}, u32[]{:S(2)}) copy-start(bf16[768,5120]{1,0:T(8,128)(2,1)} %copy.58) | copy-start | bytes 23592964
  175.3 155.3 %copy-start.6 = (s32[4]{0:T(128)S(1)}, s32[4]{0:T(128)}, u32[]{:S(2)}) copy-start(s32[4]{0:T(128)} %param.17) | copy-start | bytes 52
  273.2 5.6 %copy-start.2 = (bf16[768,768]{0,1:T(8,128)(2,1)}, bf16[768,768]{0,1:T(8,128)(2,1)S(1)}, u32[]{:S(2)}) copy-start(bf16[768,768]{0,1:T(8,128)(2,1)S(1)} %fusion.29) | copy-start | bytes 3538948
  274.3 116.0 %collective-permute-start = (bf16[768,512]{0,1:T(8,128)(2,1)}, bf16[768,512]{0,1:T(8,128)(2,1)}, u32[]{:S(2)}, u32[]{:S(2)}) collective-permute-start(bf16[768,512]{0,1:T(8,128)(2,1)} %bitcast.4), channel_id=1, source_target_pairs={{0,16},{16,32},{32,48},{48,64},{64,80},{80,96},{96,112},{112,128},... | collective-permute-start | bytes 2359304 | tf_op jit(solution)/shard_map/ppermute | solution.py:16
  276.4 116.2 %collective-permute-start.1 = (bf16[768,512]{0,1:T(8,128)(2,1)}, bf16[768,512]{0,1:T(8,128)(2,1)}, u32[]{:S(2)}, u32[]{:S(2)}) collective-permute-start(bf16[768,512]{0,1:T(8,128)(2,1)} %bitcast.4), channel_id=1, source_target_pairs={{16,0},{32,16},{48,32},{64,48},{80,64},{96,80},{112,96},{128,112},... | collective-permute-start | bytes 2359304 | tf_op jit(solution)/shard_map/ppermute | solution.py:19
  388.6 7.8 %copy-start.1 = (pred[768,2304]{0,1:T(8,128)(4,1)S(1)}, pred[768,2304]{0,1:T(8,128)(4,1)}, u32[]{:S(2)}) copy-start(pred[768,2304]{0,1:T(8,128)(4,1)} %compare_and_fusion) | copy-start | bytes 5308420
  396.4 4.2 copy-start.3
  404.7 6.9 %copy-start.5 = (bf16[768,2,1,128]{0,3,2,1:T(8,128)(2,1)S(1)}, bf16[768,2,1,128]{0,3,2,1:T(8,128)(2,1)}, u32[]{:S(2)}) copy-start(bf16[768,2,1,128]{0,3,2,1:T(8,128)(2,1)} %get-tuple-element.297) | copy-start | bytes 1179652
  404.7 7.8 %copy-start.4 = (bf16[768,2,1,128]{0,3,2,1:T(8,128)(2,1)S(1)}, bf16[768,2,1,128]{0,3,2,1:T(8,128)(2,1)}, u32[]{:S(2)}) copy-start(bf16[768,2,1,128]{0,3,2,1:T(8,128)(2,1)} %get-tuple-element.295) | copy-start | bytes 1179652
Sparse Core Ops, SparseCore 0:
  11.3 69.0 all-gather.10
  83.2 73.6 all-gather.8
  158.7 93.1 all-gather.12
  253.6 77.0 all-gather.6
  332.2 69.7 all-gather.16
  410.6 73.7 all-gather.14
where the time goes:
time: 499 us; the launch traced here: 498 us
  waiting for transfers between devices  313 us (63%)
  matrix products  72.6 us (15%)
  local copies, waits for them, and re-layouts  50.6 us (10%)
  other arithmetic  33.2 us (7%)
  between operations  14.4 us (3%)
  loops' own time  10.3 us (2%)
    all_gather x1, waiting for transfers between devices, shards(): lax.all_gather(w_qkv, 'row', axis=0, tiled=True)  76.6 us
    all_gather x1, waiting for transfers between devices, shards(): lax.all_gather(attended, 'col', axis=1, tiled=True)  71 us
    all_gather x1, waiting for transfers between devices, shards(): lax.all_gather(modulation, 'col', axis=2, tiled=True)  61.9 us
    all_gather x1, waiting for transfers between devices, shards(): slot_block = lax.all_gather(prefix_cache, 'row', axis=0, tiled=True)  51.5 us
    all_gather x1, waiting for transfers between devices, shards(): lax.all_gather(hidden_in, 'col', axis=1, tiled=True)  49.4 us
    dot_general x1, matrix products, shards(): jnp.dot(modulated, lax.all_gather(w_qkv, 'row', axis=0, tiled=True), pref...  21.3 us
    dot_general x1, matrix products, shards(): jnp.dot(onehot, full_modulation.reshape(requests, 3 * full_width), prefer...  18.8 us
    dynamic_slice x32, local copies, waits for them, and re-layouts, one_slot(): slot_data = lax.dynamic_index_in_dim(slot_block, offset, 0, keepdims=False)  17.7 us
  transfers between devices with their start and end apart: 8, of which 5 were waited for; matrix products, arithmetic and copies ran while one was open for 30% of the time, Pallas kernels for 0%

commit v1 on v0

--- a/solution.py
+++ b/solution.py
@@ -77,7 +77,9 @@
     )
     projected_qkv = jnp.dot(
         modulated,
-        lax.all_gather(w_qkv, "row", axis=0, tiled=True),
+        jnp.concatenate(
+            lax.all_to_all(jnp.stack([w_qkv] * lax.axis_size("row")), "row", 0, 0), axis=0
+        ),
         preferred_element_type=jnp.float32,
     )
     local_heads = w_qkv.shape[1] // (3 * HD)

time: 499 us -> 476 us (0.954)
  waiting for transfers between devices: 313 us -> 271 us
  starting transfers between devices: 3.87 us -> 19.7 us
    all_gather x1 -> x0, waiting for transfers between devices: 76.6 us -> none  [shards(): lax.all_gather(w_qkv, 'row', axis=0, tiled=True)]
    all_gather x1, waiting for transfers between devices: 49.4 us -> 98 us  [shards(): lax.all_gather(hidden_in, 'col', axis=1, tiled=True)]
    all_gather x1, waiting for transfers between devices: 51.5 us -> 24.7 us  [shards(): slot_block = lax.all_gather(prefix_cache, 'row', axis=0, tiled=True)]
    all_gather x1, waiting for transfers between devices: 61.9 us -> 73.6 us  [shards(): lax.all_gather(modulation, 'col', axis=2, tiled=True)]
    all_to_all x0 -> x1, starting transfers between devices: none -> 10.2 us  [shards(): lax.all_to_all(jnp.stack([w_qkv] * lax.axis_size('row')), 'row', 0, 0)]
    ppermute x1, starting transfers between devices: 2.18 us -> 7.98 us  [with_halo(): lax.ppermute(lax.slice_in_dim(block, block.shape[dim] - width, None, axis...]
  transfers between devices with their start and end apart: 8 -> 8, of which waited for: 5 -> 4; matrix products, arithmetic and copies ran while one was open for 30% -> 32% of each run, Pallas kernels for 0% -> 0%
where the time goes in v1:
time: 476 us; the launch traced here: 475 us
  waiting for transfers between devices  271 us (57%)
  matrix products  72.6 us (15%)
  local copies, waits for them, and re-layouts  54.8 us (12%)
  other arithmetic  31.9 us (7%)
  starting transfers between devices  19.7 us (4%)
  between operations  14.1 us (3%)
  loops' own time  10.3 us (2%)
    all_gather x1, waiting for transfers between devices, shards(): lax.all_gather(hidden_in, 'col', axis=1, tiled=True)  98 us
    all_gather x1, waiting for transfers between devices, shards(): lax.all_gather(modulation, 'col', axis=2, tiled=True)  73.6 us
    all_gather x1, waiting for transfers between devices, shards(): lax.all_gather(attended, 'col', axis=1, tiled=True)  73 us
    all_gather x1, waiting for transfers between devices, shards(): slot_block = lax.all_gather(prefix_cache, 'row', axis=0, tiled=True)  24.7 us
    dot_general x1, matrix products, shards(): jnp.dot(modulated, jnp.concatenate(lax.all_to_all(jnp.stack([w_qkv] * lax...  21.6 us
    dot_general x1, matrix products, shards(): jnp.dot(onehot, full_modulation.reshape(requests, 3 * full_width), prefer...  18.5 us
    dynamic_slice x32, local copies, waits for them, and re-layouts, one_slot(): slot_data = lax.dynamic_index_in_dim(slot_block, offset, 0, keepdims=False)  17.7 us
    dot_general x17, matrix products, attend(): jnp.einsum('thk,khd->thd', weights.astype(jnp.bfloat16), value_block, pre...  13.7 us
  transfers between devices with their start and end apart: 8, of which 4 were waited for; matrix products, arithmetic and copies ran while one was open for 32% of the time, Pallas kernels for 0%

profile of v1, /device:TPU:1, one launch (start us, length us, event | category | flops | bytes accessed | tf_op | source)
XLA Modules:
  0.0 474.7 jit_solution(5408674610705391747)
XLA Ops:
  7.2 1.8 copy.59
  9.1 0.7 all-gather.8.cloned.1.call-update
  9.8 4.9 %stack.2 = bf16[16,320,768]{2,1,0:T(8,128)(2,1)} broadcast(bf16[320,768]{1,0:T(8,128)(2,1)} %param.12), dimensions={1,2} | broadcast | bytes 8355840 | tf_op jit(solution)/shard_map/stack | solution.py:81
  14.7 10.2 %all-to-all-start = ((bf16[16,320,768]{2,1,0:T(8,128)(2,1)}), bf16[16,320,768]{2,1,0:T(8,128)(2,1)}, u32[]{:S(2)}, u32[]{:S(2)}) async-start(bf16[16,320,768]{2,1,0:T(8,128)(2,1)} %stack.2), calls=%async_computation | async-start | bytes 15728640 | tf_op jit(solution)/shard_map/all_to_all | solution.py:81
  28.3 2.8 compare_and_fusion
  31.1 73.6 %all-gather.10.cloned.1.call-done = bf16[48,3,5120]{0,1,2:T(4,128)(2,1)} async-done(((bf16[48,3,320]{0,1,2:T(4,128)(2,1)}), bf16[48,3,5120]{0,1,2:T(4,128)(2,1)}) %all-gather.10.cloned.1.call-update) | async-done | bytes 1474576 | tf_op jit(solution)/shard_map/all_gather | solution.py:53
  104.7 7.7 %copy.60 = bf16[48,3,5120]{2,1,0:T(4,128)(2,1)S(1)} copy(bf16[48,3,5120]{0,1,2:T(4,128)(2,1)} %all-gather.10.cloned.1.call-done) | data formatting | bytes 2949120 | tf_op jit(solution)/shard_map/all_gather | solution.py:53
  113.0 18.5 %fusion.48 = f32[768,15360]{1,0:T(8,128)} fusion(bf16[48,15360]{1,0:T(8,128)(2,1)S(1)} %bitcast.112, s32[768]{0:T(1024)S(1)} %broadcast_add_fusion.1), kind=kOutput, calls=%fused_computation.61 | convolution fusion | flops 1132498944 | bytes 48663552 | tf_op jit(solution)/shard_map/dot_general | solution.py:62
  131.5 98.0 %all-gather.8.cloned.1.call-done = bf16[768,5120]{0,1:T(8,128)(2,1)} async-done(((bf16[768,320]{0,1:T(8,128)(2,1)}), bf16[768,5120]{0,1:T(8,128)(2,1)}) %all-gather.8.cloned.1.call-update) | async-done | bytes 7864336 | tf_op jit(solution)/shard_map/all_gather | solution.py:52
  229.6 10.7 %copy.58 = bf16[768,5120]{1,0:T(8,128)(2,1)} copy(bf16[768,5120]{0,1:T(8,128)(2,1)} %all-gather.8.cloned.1.call-done) | data formatting | bytes 15728640 | tf_op jit(solution)/shard_map/all_gather | solution.py:52
  240.3 4.5 convert_reduce_fusion
  244.8 1.0 copy-done
  245.8 2.2 fusion.17
  248.0 21.6 %fusion.29 = bf16[768,768]{0,1:T(8,128)(2,1)S(1)} fusion(bf16[5120,768]{1,0:T(8,128)(2,1)} %bitcast.2, bf16[768,5120]{1,0:T(8,128)(2,1)} %copy.58, f32[768,15360]{1,0:T(8,128)} %fusion.48, f32[768]{0:T(1024)S(1)} %add_rsqrt_fusion, f32[768]{0:T(1024)S(1)} %broadcast_multiply_fusion), kind=kOutput, calls=%fused_computation.46 | convolution fusion | flops 6067912704 | bytes 48371712 | tf_op jit(solution)/shard_map/dot_general | solution.py:78
  269.6 1.0 slice.63
  270.6 1.3 collective-permute-start.1
  271.9 8.0 %collective-permute-start = (bf16[768,512]{0,1:T(8,128)(2,1)}, bf16[768,512]{0,1:T(8,128)(2,1)}, u32[]{:S(2)}, u32[]{:S(2)}) collective-permute-start(bf16[768,512]{0,1:T(8,128)(2,1)} %bitcast.5), channel_id=1, source_target_pairs={{0,16},{16,32},{32,48},{48,64},{64,80},{80,96},{96,112},{112,128},... | collective-permute-start | bytes 2359304 | tf_op jit(solution)/shard_map/ppermute | solution.py:16
  279.9 1.0 fusion.59
  281.0 24.7 %all-gather.6.cloned.1.call-done = bf16[16,256,512]{2,1,0:T(8,128)(2,1)} async-done(((bf16[1,256,512]{2,1,0:T(8,128)(2,1)}), bf16[16,256,512]{2,1,0:T(8,128)(2,1)}) %all-gather.6.cloned.1.call-update) | async-done | bytes 4194320 | tf_op jit(solution)/shard_map/all_gather | solution.py:105
  305.8 58.0 %while.20 = (s32[]{:T(128)}, f32[768,2]{0,1:T(2,128)S(1)}, f32[768,2]{0,1:T(2,128)S(1)}, f32[768,2,128]{0,2,1:T(8,128)S(1)}, s32[4]{0:T(128)S(1)}, /*index=5*/s3...) while((s32[]{:T(128)}, f32[768,2]{0,1:T(2,128)S(1)}, ...), condition=%wide.region_9.10_spmd.clone, body=%wide.region_5.9_spmd.clone.sunk | while | flops 205463824 | bytes 8100525 | solution.py:112
  305.8 1.0 constant_dynamic-slice_fusion.2
  309.4 1.0 constant_dynamic-slice_fusion.2
  313.0 1.0 constant_dynamic-slice_fusion.2
  316.6 1.0 constant_dynamic-slice_fusion.2
  320.3 1.0 constant_dynamic-slice_fusion.2
  323.9 1.0 constant_dynamic-slice_fusion.2
  327.5 1.0 constant_dynamic-slice_fusion.2
  331.1 1.0 constant_dynamic-slice_fusion.2
  334.7 1.0 constant_dynamic-slice_fusion.2
  338.4 1.0 constant_dynamic-slice_fusion.2
  342.0 1.0 constant_dynamic-slice_fusion.2
  345.6 1.0 constant_dynamic-slice_fusion.2
  349.2 1.0 constant_dynamic-slice_fusion.2
  352.9 1.0 constant_dynamic-slice_fusion.2
  356.5 1.0 constant_dynamic-slice_fusion.2
  360.1 1.0 constant_dynamic-slice_fusion.2
  363.8 1.6 copy.80
  365.4 2.3 copy.66
  367.7 2.3 copy.65
  370.0 1.6 pad_maximum_fusion
  371.6 4.2 fusion.21
  375.8 4.0 fusion.22
  379.9 5.7 %fusion.44 = bf16[768,2,128]{0,2,1:T(8,128)(2,1)} fusion(f32[2,2304,768]{2,1,0:T(8,128)S(1)} %get-tuple-element.301, f32[768,2]{0,1:T(2,128)S(1)} %max.13, pred[768,2304]{0,1:T(8,128)(4,1)S(1)} %copy-done.1, bf16[2304,2,2,128]{3,0,1,2:T(8,128)(2,1)} %copy-done.3, f32[768,2,128]{0,2,1:T(8,128)S(1)} %get-tuple-element.225, ...), kind=kOutput, calls=%fused_computation.56 | convolution fusion | flops 924450816 | bytes 18302976 | tf_op jit(solution)/shard_map/thk,khd->thd/dot_general | solution.py:40
  385.6 1.1 fusion.49
  386.7 0.9 copy.74
  387.6 0.9 copy.75
  388.6 73.0 %all-gather.12.cloned.1.call-done = bf16[768,4096]{0,1:T(8,128)(2,1)} async-done(((bf16[768,256]{0,1:T(8,128)(2,1)}), bf16[768,4096]{0,1:T(8,128)(2,1)}) %all-gather.12.cloned.1.call-update) | async-done | bytes 6291472 | tf_op jit(solution)/shard_map/all_gather | solution.py:127
  461.6 6.6 %fusion.36 = bf16[768,320]{0,1:T(8,128)(2,1)} fusion(f32[768,320]{0,1:T(8,128)S(1)} %fusion.49, bf16[4096,320]{0,1:T(8,128)(2,1)} %all-gather.14.cloned.1.call-done, bf16[768,4096]{0,1:T(8,128)(2,1)} %all-gather.12.cloned.1.call-done, bf16[768,320]{0,1:T(8,128)(2,1)} %param.10), kind=kOutput, calls=%fused_computation.50 | convolution fusion | flops 2014248960 | bytes 10878976 | tf_op jit(solution)/shard_map/dot_general | solution.py:126
  (195 shorter events, 36.3 us)
Async XLA Ops:
  7.2 97.5 %all-gather.10.cloned.1.call-start = ((), (), s32[]{:S(2)}) async-start(), calls=%async_computation.3 | async-start | bytes 5570560 | tf_op jit(solution)/shard_map/all_gather | solution.py:53
  9.1 220.5 %all-gather.8.cloned.1.call-start = ((), (), s32[]{:S(2)}) async-start(), calls=%async_computation.2 | async-start | bytes 8355840 | tf_op jit(solution)/shard_map/all_gather | solution.py:52
  14.7 11.6 %copy-start.6 = (s32[48]{0:T(128)S(1)}, s32[48]{0:T(128)}, u32[]{:S(2)}) copy-start(s32[48]{0:T(128)} %param.16) | copy-start | bytes 580
  14.7 13.4 %copy-start.7 = (s32[48]{0:T(128)S(1)}, s32[48]{0:T(128)}, u32[]{:S(2)}) copy-start(s32[48]{0:T(128)} %param.15) | copy-start | bytes 580
  14.7 233.3 %all-to-all-start = ((bf16[16,320,768]{2,1,0:T(8,128)(2,1)}), bf16[16,320,768]{2,1,0:T(8,128)(2,1)}, u32[]{:S(2)}, u32[]{:S(2)}) async-start(bf16[16,320,768]{2,1,0:T(8,128)(2,1)} %stack.2), calls=%async_computation | async-start | bytes 15728640 | tf_op jit(solution)/shard_map/all_to_all | solution.py:81
  24.9 280.9 %all-gather.6.cloned.1.call-start = ((), (), s32[]{:S(2)}) async-start(), calls=%async_computation.1 | async-start | bytes 4456448 | tf_op jit(solution)/shard_map/all_gather | solution.py:105
  25.7 362.9 %all-gather.14.cloned.1.call-start = ((), (), s32[]{:S(2)}) async-start(), calls=%async_computation.5 | async-start | bytes 2785280 | tf_op jit(solution)/shard_map/all_gather | solution.py:125
  26.2 435.4 %all-gather.12.cloned.1.call-start = ((), (), s32[]{:S(2)}) async-start(), calls=%async_computation.4 | async-start | bytes 6684672 | tf_op jit(solution)/shard_map/all_gather | solution.py:127
  240.3 5.5 %copy-start = (bf16[768,5120]{1,0:T(8,128)(2,1)S(1)}, bf16[768,5120]{1,0:T(8,128)(2,1)}, u32[]{:S(2)}) copy-start(bf16[768,5120]{1,0:T(8,128)(2,1)} %copy.58) | copy-start | bytes 23592964
  247.9 57.8 %copy-start.8 = (s32[4]{0:T(128)S(1)}, s32[4]{0:T(128)}, u32[]{:S(2)}) copy-start(s32[4]{0:T(128)} %param.17) | copy-start | bytes 52
  269.6 11.3 %copy-start.2 = (bf16[768,768]{0,1:T(8,128)(2,1)}, bf16[768,768]{0,1:T(8,128)(2,1)S(1)}, u32[]{:S(2)}) copy-start(bf16[768,768]{0,1:T(8,128)(2,1)S(1)} %fusion.29) | copy-start | bytes 3538948
  270.6 94.8 %collective-permute-start.1 = (bf16[768,512]{0,1:T(8,128)(2,1)}, bf16[768,512]{0,1:T(8,128)(2,1)}, u32[]{:S(2)}, u32[]{:S(2)}) collective-permute-start(bf16[768,512]{0,1:T(8,128)(2,1)} %bitcast.5), channel_id=1, source_target_pairs={{16,0},{32,16},{48,32},{64,48},{80,64},{96,80},{112,96},{128,112},... | collective-permute-start | bytes 2359304 | tf_op jit(solution)/shard_map/ppermute | solution.py:19
  271.9 95.8 %collective-permute-start = (bf16[768,512]{0,1:T(8,128)(2,1)}, bf16[768,512]{0,1:T(8,128)(2,1)}, u32[]{:S(2)}, u32[]{:S(2)}) collective-permute-start(bf16[768,512]{0,1:T(8,128)(2,1)} %bitcast.5), channel_id=1, source_target_pairs={{0,16},{16,32},{32,48},{48,64},{64,80},{80,96},{96,112},{112,128},... | collective-permute-start | bytes 2359304 | tf_op jit(solution)/shard_map/ppermute | solution.py:16
  363.7 7.8 %copy-start.1 = (pred[768,2304]{0,1:T(8,128)(4,1)S(1)}, pred[768,2304]{0,1:T(8,128)(4,1)}, u32[]{:S(2)}) copy-start(pred[768,2304]{0,1:T(8,128)(4,1)} %compare_and_fusion) | copy-start | bytes 5308420
  371.6 4.2 copy-start.3
  379.8 6.9 %copy-start.5 = (bf16[768,2,1,128]{0,3,2,1:T(8,128)(2,1)S(1)}, bf16[768,2,1,128]{0,3,2,1:T(8,128)(2,1)}, u32[]{:S(2)}) copy-start(bf16[768,2,1,128]{0,3,2,1:T(8,128)(2,1)} %get-tuple-element.297) | copy-start | bytes 1179652
  379.9 7.8 %copy-start.4 = (bf16[768,2,1,128]{0,3,2,1:T(8,128)(2,1)S(1)}, bf16[768,2,1,128]{0,3,2,1:T(8,128)(2,1)}, u32[]{:S(2)}) copy-start(bf16[768,2,1,128]{0,3,2,1:T(8,128)(2,1)} %get-tuple-element.295) | copy-start | bytes 1179652
Sparse Core Ops, SparseCore 0:
  11.3 93.3 all-gather.9
  107.5 122.0 all-gather.7
  231.4 74.3 all-gather.5
  307.3 71.9 all-gather.13
  385.7 75.8 all-gather.11
